TPU v7x, 32 devices: a whole 2x2x4 slice. The times are simulated.
32 devices in a mesh: grp: 2 (over x), slc: 16 (over z, y, core).
Axes of the slice: x: 2, y: 2, z: 4, core: 2. Of those that a mesh axis runs over, the one named last changes fastest.
Arguments:
- bitstrings: int32 [1024], P('grp'), parts along dimension 0, may hold values from 0 to 511, as said below
- tree_order: int32 [12], P('grp'), parts along dimension 0, may hold values from 0 to 5, each once
- owners: int32 [12], P('grp'), parts along dimension 0, may hold values from 0 to 15
- slice_assign: int32 [64, 6], P(('grp', 'slc')), parts along dimension 0, may hold values from 0 to 63
- boundary: bfloat16 [1024, 4096], P('grp'), parts along dimension 0, may hold values from -6 to 6
- branch_pool: bfloat16 [32, 64, 4096], P(('grp', 'slc')), parts along dimension 0, may hold values from -0.75 to 0.75
- slice_tensors: bfloat16 [12, 64, 4096], P('grp'), parts along dimension 0, may hold values from -3 to 3
- closing: bfloat16 [8192, 128], P('grp'), parts along dimension 0, may hold values from -0.09375 to 0.09375
Outputs:
- amplitudes: float32 [1024, 128], P(('grp', 'slc')), parts along dimension 0
There are 2 independent parts, one for each index of `grp`. A program takes and returns all parts, laid end to end along the dimension named above; each array names one. Nothing has to cross between parts.
Inputs may be any that keep to these rules, and one draw needn't show every extreme that they name: `bitstrings`: 512 distinct configurations. `tree_order`: a permutation of the sections.
All inputs are finite; a program needn't handle non-finite values.
Results may differ from a plain program's by a relative error of at most 0.0075.
Values may be sent and summed in bfloat16 or wider, within the bound.
A program may use at most 128 MiB of HBM per device.

v0:
```python
import math
import jax
import jax.numpy as jnp
from jax import lax
from jax.sharding import PartitionSpec as P


def spread(block, axis, owner):
    block = jnp.where(lax.axis_index(axis) == owner, block, jnp.zeros_like(block))
    return lax.psum(block, axis)


def local(
    bitstrings, tree_order, owners, slice_assign, boundary, branch_pool, slice_tensors, closing
):
    group_count = lax.axis_size("slc")
    my_index = lax.axis_index("slc")
    slice_count = slice_assign.shape[0]
    bond_dim = branch_pool.shape[1]
    pair_dim = branch_pool.shape[2]
    row_total = bitstrings.shape[0]
    section_count = tree_order.shape[0]
    starts = jnp.take(boundary, bitstrings, axis=0)
    states = jnp.broadcast_to(starts[None], (slice_count, row_total, pair_dim))
    own_branch = branch_pool[0]
    for section_idx in range(section_count):
        branch = spread(own_branch, "slc", owners[section_idx])
        product = jnp.einsum(
            "srab,acb->srcb",
            states.reshape(slice_count, row_total, bond_dim, bond_dim),
            branch.reshape(bond_dim, bond_dim, bond_dim),
            preferred_element_type=jnp.float32,
        )
        table = lax.dynamic_index_in_dim(slice_tensors, tree_order[section_idx], 0, keepdims=False)
        factor = jnp.take(table, slice_assign[:, section_idx], axis=0).astype(jnp.float32)
        states = (product.reshape(slice_count, row_total, pair_dim) * factor[:, None, :]).astype(
            jnp.bfloat16
        )
    inverse = 1.0 / math.sqrt(slice_count * group_count)
    share_rows = row_total // group_count
    partial_amps = jnp.einsum("srw,wo->ro", states, closing, preferred_element_type=jnp.float32)
    totals = lax.psum(partial_amps, "slc")
    summed = lax.dynamic_slice_in_dim(totals, my_index * share_rows, share_rows, 0)
    return summed * inverse


def solution(mesh):
    return jax.shard_map(
        local,
        mesh=mesh,
        in_specs=(
            P("grp"),
            P("grp"),
            P("grp"),
            P(("grp", "slc"), None),
            P("grp", None),
            P(("grp", "slc"), None, None),
            P("grp", None, None),
            P("grp", None),
        ),
        out_specs=P(("grp", "slc"), None),
        check_vma=False,
    )
```

profile of v0, /device:TPU:0, one launch (start us, length us, event | category | flops | bytes accessed | tf_op | source)
XLA Modules:
  0.0 318.7 jit_solution(11319033203107848922)
XLA Ops:
  6.5 1.5 fusion.25
  11.9 2.4 broadcast_select_fusion.6
  14.3 2.1 reshape.99
  16.3 2.9 copy.34
  19.3 2.1 reshape.102
  21.3 2.9 copy.37
  24.2 2.1 reshape.101
  26.3 2.9 copy.36
  29.2 2.1 reshape.100
  31.3 2.9 copy.35
  34.2 1.1 reshape.104
  35.3 2.9 copy.39
  38.2 1.1 reshape.103
  39.4 2.9 copy.38
  42.3 0.2 all-reduce.4.cloned.1.call-start
  42.6 0.7 fusion.24
  50.8 0.3 slice_reduce_fusion.1
  55.0 3.2 dynamic-slice_bitcast_fusion.1
  58.2 1.7 gather_fusion.5
  60.0 0.1 reshape.115
  60.1 0.1 copy.46
  60.2 1.7 gather_fusion.4
  62.0 0.1 reshape.114
  62.1 0.1 copy.45
  62.2 0.6 gather_fusion.3
  62.9 0.1 reshape.113
  63.0 0.1 copy.44
  63.1 0.6 gather_fusion.2
  63.7 0.1 reshape.112
  63.8 0.1 copy.43
  63.9 0.6 gather_fusion.1
  64.6 0.1 reshape.111
  64.7 0.1 copy.42
  64.8 0.6 gather_fusion.6
  65.5 0.1 reshape.116
  65.6 0.1 copy.47
  65.7 11.4 %gather_fusion = bf16[512,4096]{1,0:T(8,128)(2,1)} fusion(bf16[512,4096]{1,0:T(8,128)(2,1)} %param.14, s32[1024]{0:T(1024)S(1)} %pad_clamp_fusion.6), kind=kCustom, calls=%fused_computation.6 | custom fusion | bytes 8390656 | tf_op jit(solution)/shard_map/jit(_take)/gather | solution.py:23
  77.1 6.5 %copy.40 = bf16[512,4096]{0,1:T(8,128)(2,1)} copy(bf16[512,4096]{1,0:T(8,128)(2,1)} %gather_fusion) | data formatting | bytes 8388608 | tf_op jit(solution)/shard_map/jit(_take)/gather | solution.py:23
  83.6 2.7 broadcast_select_fusion
  86.3 4.4 %copy.41 = bf16[512,64,64]{0,1,2:T(8,128)(2,1)} copy(bf16[512,64,64]{0,2,1:T(8,128)(2,1)S(1)} %broadcast_select_fusion) | data formatting | bytes 8388608 | tf_op jit(solution)/shard_map/jit(_take)/select_n | solution.py:23
  90.7 94.3 %all-reduce.6.cloned.1.call-done = (bf16[64,64,64]{0,1,2:T(8,128)(2,1)}, bf16[64,64,64]{0,1,2:T(8,128)(2,1)}, bf16[64,64,64]{0,1,2:T(8,128)(2,1)}, bf16[64,64,64...) async-done(((bf16[64,64,64]{0,1,2:T(8,128)(2,1)}, bf16[64,64,64]{0,1,2:T(8,128)(2,1)}, bf16[64,64,64]{0,1,2:T(8,128)(2,1)}, ...) | async-done | bytes 3145744 | tf_op jit(solution)/shard_map/psum | solution.py:10
  185.0 8.7 %fusion.4 = bf16[2,512,64,64]{1,2,0,3:T(8,128)(2,1)} fusion(f32[2,64,64]{1,0,2:T(2,128)S(1)} %copy.43, f32[2,64,64]{1,0,2:T(2,128)S(1)} %copy.42, bf16[512,64,64]{0,1,2:T(8,128)(2,1)} %copy.41, bf16[64,64,64]{0,1,2:T(8,128)(2,1)} %get-tuple-element.12, bf16[64,64,64]{0,1,2:T(8,128)(2,1)} %get-tuple-element.13), kind=kOutput, calls=%fused_computation.16 | convolution fusion | flops 1090519040 | bytes 13697024 | tf_op jit(solution)/shard_map/srab,acb->srcb/dot_general | solution.py:28
  193.7 9.8 %fusion.2 = bf16[2,512,64,64]{1,2,0,3:T(8,128)(2,1)} fusion(f32[2,64,64]{1,0,2:T(2,128)S(1)} %copy.45, bf16[2,512,64,64]{1,2,0,3:T(8,128)(2,1)} %fusion.4, f32[2,64,64]{1,0,2:T(2,128)S(1)} %copy.44, bf16[64,64,64]{0,1,2:T(8,128)(2,1)S(1)} %copy-done.1, bf16[64,64,64]{0,1,2:T(8,128)(2,1)S(1)} %copy-done.2), kind=kOutput, calls=%fused_computation.12 | convolution fusion | flops 1090519040 | bytes 17891328 | tf_op jit(solution)/shard_map/srab,acb->srcb/dot_general | solution.py:28
  203.5 10.4 %convert_reduce_fusion = bf16[512,64,64]{0,1,2:T(8,128)(2,1)} fusion(f32[2,64,64]{1,0,2:T(2,128)S(1)} %copy.47, bf16[2,512,64,64]{1,2,0,3:T(8,128)(2,1)} %fusion.2, f32[2,64,64]{1,0,2:T(2,128)S(1)} %copy.46, bf16[64,64,64]{0,1,2:T(8,128)(2,1)} %get-tuple-element.16, bf16[64,64,64]{0,1,2:T(8,128)(2,1)} %get-tuple-element.17), kind=kOutput, calls=%fused_computation.19 | convolution fusion | flops 1096810496 | bytes 13697024 | tf_op jit(solution)/shard_map/srab,acb->srcb/dot_general | solution.py:28
  213.9 4.5 %copy.48 = bf16[512,64,64]{0,2,1:T(8,128)(2,1)S(1)} copy(bf16[512,64,64]{0,1,2:T(8,128)(2,1)} %convert_reduce_fusion) | data formatting | bytes 8388608 | tf_op jit(solution)/shard_map/srw,wo->ro/reduce_sum | solution.py:41
  218.4 2.0 fusion.26
  220.5 90.1 %all-reduce.4.cloned.1.call-done = f32[512,128]{1,0:T(8,128)} async-done(((f32[512,128]{1,0:T(8,128)}), f32[512,128]{1,0:T(8,128)}) %all-reduce.4.cloned.1.call-update) | async-done | bytes 262160 | tf_op jit(solution)/shard_map/psum | solution.py:42
  310.5 1.3 dynamic-slice_multiply_fusion
  (36 shorter events, 0.7 us)
Async XLA Ops:
  6.5 211.9 %copy-start = (bf16[4096,128]{1,0:T(8,128)(2,1)S(1)}, bf16[4096,128]{1,0:T(8,128)(2,1)}, u32[]{:S(2)}) copy-start(bf16[4096,128]{1,0:T(8,128)(2,1)} %param.17) | copy-start | bytes 3145732
  6.5 178.4 %all-reduce.6.cloned.1.call-start = ((), (), s32[]{:S(2)}) async-start(), calls=%async_computation.1 | async-start | bytes 12582912 | tf_op jit(solution)/shard_map/psum | solution.py:10
  29.2 13.4 %copy-start.4 = (s32[6]{0:T(128)S(1)}, s32[6]{0:T(128)}, u32[]{:S(2)}) copy-start(s32[6]{0:T(128)} %param.11) | copy-start | bytes 76
  29.2 21.6 %copy-start.3 = (s32[2,6]{1,0:T(2,128)S(1)}, s32[2,6]{1,0:T(2,128)}, u32[]{:S(2)}) copy-start(s32[2,6]{1,0:T(2,128)} %param.13) | copy-start | bytes 148
  39.4 26.3 %copy-start.5 = (s32[512]{0:T(512)S(1)}, s32[512]{0:T(512)}, u32[]{:S(2)}) copy-start(s32[512]{0:T(512)} %param.10) | copy-start | bytes 6148
  42.3 268.2 %all-reduce.4.cloned.1.call-start = ((), (), s32[]{:S(2)}) async-start(), calls=%async_computation | async-start | bytes 524288 | tf_op jit(solution)/shard_map/psum | solution.py:42
  185.0 8.7 %copy-start.1 = (bf16[64,64,64]{0,1,2:T(8,128)(2,1)S(1)}, bf16[64,64,64]{0,1,2:T(8,128)(2,1)}, u32[]{:S(2)}) copy-start(bf16[64,64,64]{0,1,2:T(8,128)(2,1)} %get-tuple-element.14) | copy-start | bytes 1572868
  185.0 8.7 %copy-start.2 = (bf16[64,64,64]{0,1,2:T(8,128)(2,1)S(1)}, bf16[64,64,64]{0,1,2:T(8,128)(2,1)}, u32[]{:S(2)}) copy-start(bf16[64,64,64]{0,1,2:T(8,128)(2,1)} %get-tuple-element.15) | copy-start | bytes 1572868
Sparse Core Ops, SparseCore 0:
  42.4 142.4 all-reduce.5
  220.6 89.9 all-reduce.3
where the time goes:
time: 320 us; the launch traced here: 319 us
  waiting for transfers between devices  184 us (58%)
  local copies, waits for them, and re-layouts  67.4 us (21%)
  matrix products  30.9 us (10%)
  between operations  28.8 us (9%)
  other arithmetic  7.02 us (2%)
    psum x1, waiting for transfers between devices, spread(): return lax.psum(block, axis)  94.3 us
    psum x1, waiting for transfers between devices, local(): totals = lax.psum(partial_amps, 'slc')  90.1 us
    dot_general x3, matrix products, local(): jnp.einsum('srab,acb->srcb', states.reshape(slice_count, row_total, bond_...  28.9 us
    reshape x12, local copies, waits for them, and re-layouts, local(): branch.reshape(bond_dim, bond_dim, bond_dim)  28 us
    gather x2, local copies, waits for them, and re-layouts, local(): starts = jnp.take(boundary, bitstrings, axis=0)  17.9 us
  transfers between devices with their start and end apart: 2, of which 2 were waited for; matrix products, arithmetic and copies ran while one was open for 11% of the time, Pallas kernels for 0%

commit v1 on v0

--- a/solution.py
+++ b/solution.py
@@ -7,7 +7,11 @@
 
 def spread(block, axis, owner):
     block = jnp.where(lax.axis_index(axis) == owner, block, jnp.zeros_like(block))
-    return lax.psum(block, axis)
+
+    def bring_stages_all_by_axis(sheet):
+        return jnp.sum(lax.all_gather(sheet, axis), 0)
+
+    return bring_stages_all_by_axis(block)
 
 
 def local(

time: 320 us -> 615 us (1.92)
  waiting for transfers between devices: 184 us -> 440 us
  other arithmetic: 7.02 us -> 38.9 us
    all_gather x0 -> x6, waiting for transfers between devices: none -> 348 us  [bring_stages_all_by_axis(): return jnp.sum(lax.all_gather(sheet, axis), 0)]
    psum x1 -> x0, waiting for transfers between devices: 94.3 us -> none  [spread(): return lax.psum(block, axis)]
    reduce_sum x0 -> x6, other arithmetic: none -> 31.6 us  [bring_stages_all_by_axis(): return jnp.sum(lax.all_gather(sheet, axis), 0)]
  transfers between devices with their start and end apart: 2 -> 7, of which waited for: 2 -> 7; matrix products, arithmetic and copies ran while one was open for 11% -> 15% of each run, Pallas kernels for 0% -> 0%
where the time goes in v1:
time: 615 us; the launch traced here: 612 us
  waiting for transfers between devices  440 us (72%)
  local copies, waits for them, and re-layouts  72.6 us (12%)
  other arithmetic  38.9 us (6%)
  matrix products  30.7 us (5%)
  between operations  29.4 us (5%)
    all_gather x6, waiting for transfers between devices, bring_stages_all_by_axis(): return jnp.sum(lax.all_gather(sheet, axis), 0)  348 us
    psum x1, waiting for transfers between devices, local(): totals = lax.psum(partial_amps, 'slc')  88.5 us
    reduce_sum x6, other arithmetic, bring_stages_all_by_axis(): return jnp.sum(lax.all_gather(sheet, axis), 0)  31.6 us
    reshape x12, local copies, waits for them, and re-layouts, local(): branch.reshape(bond_dim, bond_dim, bond_dim)  31.1 us
    dot_general x3, matrix products, local(): jnp.einsum('srab,acb->srcb', states.reshape(slice_count, row_total, bond_...  28.8 us
    gather x2, local copies, waits for them, and re-layouts, local(): starts = jnp.take(boundary, bitstrings, axis=0)  18.3 us
  transfers between devices with their start and end apart: 7, of which 7 were waited for; matrix products, arithmetic and copies ran while one was open for 15% of the time, Pallas kernels for 0%

profile of v1, /device:TPU:0, one launch (start us, length us, event | category | flops | bytes accessed | tf_op | source)
XLA Modules:
  0.0 611.6 jit_solution(12091295502555042793)
XLA Ops:
  6.5 1.5 fusion.16
  11.9 2.8 broadcast_select_fusion.1
  14.7 0.7 all-gather.15.cloned.1.call-update
  15.4 0.7 all-gather.13.cloned.1.call-update
  17.9 1.6 fusion.15
  31.1 1.2 slice_reduce_fusion.1
  32.3 3.1 dynamic-slice_bitcast_fusion.1
  35.3 1.7 gather_fusion.1
  37.4 1.7 gather_fusion.2
  39.4 11.7 %gather_fusion = bf16[512,4096]{1,0:T(8,128)(2,1)} fusion(bf16[512,4096]{1,0:T(8,128)(2,1)} %param.14, s32[1024]{0:T(1024)S(1)} %pad_clamp_fusion.6), kind=kCustom, calls=%fused_computation.6 | custom fusion | bytes 8390656 | tf_op jit(solution)/shard_map/jit(_take)/gather | solution.py:27
  51.1 6.7 %copy.34 = bf16[512,4096]{0,1:T(8,128)(2,1)} copy(bf16[512,4096]{1,0:T(8,128)(2,1)} %gather_fusion) | data formatting | bytes 8388608 | tf_op jit(solution)/shard_map/jit(_take)/gather | solution.py:27
  57.7 2.6 broadcast_select_fusion
  60.4 4.4 copy.35
  64.8 0.6 gather_fusion.3
  65.7 0.6 gather_fusion.4
  66.6 0.6 gather_fusion.5
  67.5 0.6 gather_fusion.6
  68.4 23.4 %all-gather.17.cloned.1.call-done = bf16[16,64,4096]{2,1,0:T(8,128)(2,1)} async-done(((bf16[1,64,4096]{2,1,0:T(8,128)(2,1)}), bf16[16,64,4096]{2,1,0:T(8,128)(2,1)}) %all-gather.17.cloned.1.call-update) | async-done | bytes 8388624 | tf_op jit(solution)/shard_map/all_gather | solution.py:12
  91.8 5.0 reduce_sum.88
  96.8 1.1 reshape.86
  97.9 3.4 copy.49
  101.4 65.5 %all-gather.15.cloned.1.call-done = bf16[16,64,4096]{2,1,0:T(8,128)(2,1)} async-done(((bf16[1,64,4096]{2,1,0:T(8,128)(2,1)}), bf16[16,64,4096]{2,1,0:T(8,128)(2,1)}) %all-gather.15.cloned.1.call-update) | async-done | bytes 8388624 | tf_op jit(solution)/shard_map/all_gather | solution.py:12
  166.9 5.0 reduce_sum.87
  171.9 1.1 reshape.85
  173.0 2.9 copy.50
  176.0 66.0 %all-gather.13.cloned.1.call-done = bf16[16,64,4096]{2,1,0:T(8,128)(2,1)} async-done(((bf16[1,64,4096]{2,1,0:T(8,128)(2,1)}), bf16[16,64,4096]{2,1,0:T(8,128)(2,1)}) %all-gather.13.cloned.1.call-update) | async-done | bytes 8388624 | tf_op jit(solution)/shard_map/all_gather | solution.py:12
  242.0 5.0 reduce_sum.86
  247.0 1.1 reshape.84
  248.1 2.2 copy.51
  250.3 66.6 %all-gather.11.cloned.1.call-done = bf16[16,64,4096]{2,1,0:T(8,128)(2,1)} async-done(((bf16[1,64,4096]{2,1,0:T(8,128)(2,1)}), bf16[16,64,4096]{2,1,0:T(8,128)(2,1)}) %all-gather.11.cloned.1.call-update) | async-done | bytes 8388624 | tf_op jit(solution)/shard_map/all_gather | solution.py:12
  316.9 5.0 reduce_sum.85
  321.9 2.1 reshape.83
  324.0 3.5 copy.52
  327.5 64.3 %all-gather.9.cloned.1.call-done = bf16[16,64,4096]{2,1,0:T(8,128)(2,1)} async-done(((bf16[1,64,4096]{2,1,0:T(8,128)(2,1)}), bf16[16,64,4096]{2,1,0:T(8,128)(2,1)}) %all-gather.9.cloned.1.call-update) | async-done | bytes 8388624 | tf_op jit(solution)/shard_map/all_gather | solution.py:12
  391.8 5.9 reduce_sum.84
  397.7 2.7 reshape.82
  400.4 4.0 copy.53
  404.4 62.3 %all-gather.7.cloned.1.call-done = bf16[16,64,4096]{2,1,0:T(8,128)(2,1)} async-done(((bf16[1,64,4096]{2,1,0:T(8,128)(2,1)}), bf16[16,64,4096]{2,1,0:T(8,128)(2,1)}) %all-gather.7.cloned.1.call-update) | async-done | bytes 8388624 | tf_op jit(solution)/shard_map/all_gather | solution.py:12
  466.8 5.9 reduce_sum.83
  472.6 2.8 reshape.81
  475.4 4.0 copy.54
  479.4 8.6 %fusion.4 = bf16[2,512,64,64]{1,2,0,3:T(8,128)(2,1)} fusion(bf16[64,64,64,1]{0,1,3,2:T(8,128)(2,1)} %copy.50, f32[2,64,64]{1,0,2:T(2,128)S(1)} %copy.39, bf16[64,64,64,1]{0,1,3,2:T(8,128)(2,1)} %copy.49, f32[2,64,64]{1,0,2:T(2,128)S(1)} %copy.37, bf16[512,64,64]{0,1,2:T(8,128)(2,1)} %copy.35), kind=kOutput, calls=%fused_computation.16 | convolution fusion | flops 1090519040 | bytes 13697024 | tf_op jit(solution)/shard_map/srab,acb->srcb/dot_general | solution.py:32
  488.0 10.0 %fusion.2 = bf16[2,512,64,64]{1,2,0,3:T(8,128)(2,1)} fusion(bf16[64,64,64,1]{0,1,3,2:T(8,128)(2,1)S(1)} %copy.52, f32[2,64,64]{1,0,2:T(2,128)S(1)} %copy.43, bf16[64,64,64,1]{0,1,3,2:T(8,128)(2,1)S(1)} %copy.51, bf16[2,512,64,64]{1,2,0,3:T(8,128)(2,1)} %fusion.4, f32[2,64,64]{1,0,2:T(2,128)S(1)} %copy.41), kind=kOutput, calls=%fused_computation.12 | convolution fusion | flops 1090519040 | bytes 17891328 | tf_op jit(solution)/shard_map/srab,acb->srcb/dot_general | solution.py:32
  498.0 10.2 %convert_reduce_fusion = bf16[512,64,64]{0,1,2:T(8,128)(2,1)} fusion(f32[2,64,64]{1,0,2:T(2,128)S(1)} %copy.47, bf16[64,64,64,1]{0,1,3,2:T(8,128)(2,1)} %copy.54, bf16[64,64,64,1]{0,1,3,2:T(8,128)(2,1)} %copy.53, bf16[2,512,64,64]{1,2,0,3:T(8,128)(2,1)} %fusion.2, f32[2,64,64]{1,0,2:T(2,128)S(1)} %copy.45), kind=kOutput, calls=%fused_computation.19 | convolution fusion | flops 1096810496 | bytes 13697024 | tf_op jit(solution)/shard_map/srab,acb->srcb/dot_general | solution.py:32
  508.1 4.5 copy.48
  512.7 2.0 fusion.17
  514.7 88.5 %all-reduce.2.cloned.1.call-done = f32[512,128]{1,0:T(8,128)} async-done(((f32[512,128]{1,0:T(8,128)}), f32[512,128]{1,0:T(8,128)}) %all-reduce.2.cloned.1.call-update) | async-done | bytes 262160 | tf_op jit(solution)/shard_map/psum | solution.py:46
  603.2 1.3 dynamic-slice_multiply_fusion
  (49 shorter events, 3.6 us)
Async XLA Ops:
  6.5 506.1 %copy-start = (bf16[4096,128]{1,0:T(8,128)(2,1)S(1)}, bf16[4096,128]{1,0:T(8,128)(2,1)}, u32[]{:S(2)}) copy-start(bf16[4096,128]{1,0:T(8,128)(2,1)} %param.17) | copy-start | bytes 3145732
  6.5 32.8 %copy-start.1 = (s32[512]{0:T(512)S(1)}, s32[512]{0:T(512)}, u32[]{:S(2)}) copy-start(s32[512]{0:T(512)} %param.10) | copy-start | bytes 6148
  6.5 85.3 %all-gather.17.cloned.1.call-start = ((), (), s32[]{:S(2)}) async-start(), calls=%async_computation.5 | async-start | bytes 8912896 | tf_op jit(solution)/shard_map/all_gather | solution.py:12
  14.6 152.3 %all-gather.15.cloned.1.call-start = ((), (), s32[]{:S(2)}) async-start(), calls=%async_computation.4 | async-start | bytes 8912896 | tf_op jit(solution)/shard_map/all_gather | solution.py:12
  15.4 226.6 %all-gather.13.cloned.1.call-start = ((), (), s32[]{:S(2)}) async-start(), calls=%async_computation.3 | async-start | bytes 8912896 | tf_op jit(solution)/shard_map/all_gather | solution.py:12
  16.1 300.8 %all-gather.11.cloned.1.call-start = ((), (), s32[]{:S(2)}) async-start(), calls=%async_computation.2 | async-start | bytes 8912896 | tf_op jit(solution)/shard_map/all_gather | solution.py:12
  16.7 375.1 %all-gather.9.cloned.1.call-start = ((), (), s32[]{:S(2)}) async-start(), calls=%async_computation.1 | async-start | bytes 8912896 | tf_op jit(solution)/shard_map/all_gather | solution.py:12
  17.3 449.5 %all-gather.7.cloned.1.call-start = ((), (), s32[]{:S(2)}) async-start(), calls=%async_computation | async-start | bytes 8912896 | tf_op jit(solution)/shard_map/all_gather | solution.py:12
  17.9 585.3 %all-reduce.2.cloned.1.call-start = ((), (), s32[]{:S(2)}) async-start(), calls=%async_computation.6 | async-start | bytes 524288 | tf_op jit(solution)/shard_map/psum | solution.py:46
Sparse Core Ops, SparseCore 0:
  14.8 77.0 all-gather.16
  94.0 72.8 all-gather.14
  169.1 72.8 all-gather.12
  244.0 72.8 all-gather.10
  318.9 72.8 all-gather.8
  393.9 72.8 all-gather.6
  514.8 88.3 all-reduce.1
